TPU v7x, 768 devices: a whole 4x8x12 slice. The times are simulated.
768 devices in a mesh: circ: 24 (over z, x_hi), radax: 32 (over y, x_lo, core).
Axes of the slice: x: 4 (x_hi: 2, x_lo: 2; x = x_hi * 2 + x_lo), y: 8, z: 12, core: 2. Of those that a mesh axis runs over, the one named last changes fastest.
Arguments:
- right_side: float32 [12288, 8192], P('circ', 'radax'), may hold values from -150 to 150
- coef_rotor: float32 [12288, 8192], P('circ', 'radax'), may hold values from 1.5 to 15
- coef_stator: float32 [12288, 8192], P('circ', 'radax'), may hold values from 1.5 to 15
- mortar_rows: int32 [12288], P('circ'), may hold values from 0 to 12287, as said below
- mortar_weight: float32 [12288], P('circ'), may hold values from 0.1 to 0.9
Outputs:
- solution_field: float32 [12288, 8192], P('circ', 'radax')
- residual: float32 [12288, 8192], P('circ', 'radax')
Inputs may be any that keep to these rules, and one draw needn't show every extreme that they name: (mortar_rows[s] - s - 1280) taken modulo 12288 lies in -3 to 3, and both ends occur.
All inputs are finite; a program needn't handle non-finite values.
Results may differ from a plain program's by a relative error of at most 0.0002.
Values sent between devices are 32-bit elements; how exact they have to be, the bound alone decides.
A program may use at most 32 MiB of HBM per device.

v0:
```python
import jax
import jax.numpy as jnp
from jax import lax
from jax.sharding import Mesh
from jax.sharding import PartitionSpec as P

W = 256
REACH = 3
SLIDE = 1280
CIRC = ("circ_0", "circ_1")
CIRC_RADAX = ("circ_0", "circ_1", "radax_0", "radax_1", "radax_2")
RADAX = ("radax_0", "radax_1", "radax_2")


def with_halo(cells, sides, width):
    for axis, dim in sides:
        count = lax.axis_size(axis)
        head = lax.slice_in_dim(cells, 0, width, axis=dim)
        tail = lax.slice_in_dim(cells, cells.shape[dim] - width, cells.shape[dim], axis=dim)
        cells = jnp.concatenate(
            [
                lax.ppermute(tail, axis, [(i, (i + 1) % count) for i in range(count)]),
                cells,
                lax.ppermute(head, axis, [((i + 1) % count, i) for i in range(count)]),
            ],
            axis=dim,
        )
    return cells


def shifted(block, axis, distance):
    devices = range(lax.axis_size(axis))
    route = [((i - distance) % len(devices), i) for i in devices]
    return lax.ppermute(block, axis, route)


def over_axes(shard, axes):
    for axis in axes:
        shard = lax.psum(shard, axis)
    return shard


def local(right_side, coef_rotor, coef_stator, mortar_rows, mortar_weight):
    row_count = right_side.shape[0]
    col_count = right_side.shape[1]
    cycle_size = lax.axis_size(CIRC)
    total_rows = row_count * cycle_size

    def stencil(grid_field, coef):
        padded = with_halo(grid_field, ((CIRC, 0),), 1)
        blocks = grid_field.reshape(grid_field.shape[0], col_count // W, W)
        side_pad = jnp.pad(blocks, ((0, 0), (0, 0), (1, 1)))
        beside = (side_pad[:, :, :-2] + side_pad[:, :, 2:]).reshape(grid_field.shape)
        return coef * grid_field - 0.25 * (padded[:-2] + padded[2:] + beside)

    start_off = SLIDE - REACH
    span_rows = row_count + 2 * REACH + 1
    owners = list(range(start_off // row_count, (start_off + span_rows - 1) // row_count + 1))
    bounds = [
        (
            max(0, start_off - shift_by * row_count),
            min(row_count, start_off - shift_by * row_count + span_rows),
        )
        for shift_by in owners
    ]
    anchor = lax.axis_index(CIRC) * row_count + start_off
    local_idx = jnp.mod(mortar_rows - anchor, total_rows)
    after_idx = local_idx + 1
    weight = mortar_weight[:, None]

    def project(trace):
        pieces = []
        for shift_by, (low_row, high_row) in zip(owners, bounds):
            outgoing = trace[low_row:high_row]
            arrived = shifted(outgoing, CIRC, -shift_by)
            pieces.append(arrived)
        window = jnp.concatenate(pieces, axis=0)
        return weight * window[local_idx] + (1.0 - weight) * window[after_idx]

    def give_back(response):
        collect = jnp.zeros((span_rows, col_count), jnp.float32)
        collect = collect.at[local_idx].add(weight * response)
        collect = collect.at[after_idx].add((1.0 - weight) * response)
        summed = jnp.zeros((row_count, col_count), jnp.float32)
        begin = 0
        for shift_by, (low_row, high_row) in zip(owners, bounds):
            portion = collect[begin : begin + high_row - low_row]
            begin = begin + high_row - low_row
            arrived = shifted(portion, CIRC, shift_by)
            summed = summed + jnp.pad(arrived, ((low_row, row_count - high_row), (0, 0)))
        return summed

    def operator(trace):
        return stencil(trace, coef_rotor) + give_back(stencil(project(trace), coef_stator))

    image = operator(right_side)
    cross_one, gram_pp = (
        over_axes(jnp.sum(right_side * image), CIRC_RADAX),
        over_axes(jnp.sum(image * image), CIRC_RADAX),
    )
    second = operator(image)
    gram_pq, gram_qq, cross_two = (
        over_axes(jnp.sum(image * second), CIRC_RADAX),
        over_axes(jnp.sum(second * second), CIRC_RADAX),
        over_axes(jnp.sum(right_side * second), CIRC_RADAX),
    )
    determinant = gram_pp * gram_qq - gram_pq * gram_pq
    coeff_one = (gram_qq * cross_one - gram_pq * cross_two) / determinant
    coeff_two = (gram_pp * cross_two - gram_pq * cross_one) / determinant
    solution_field = coeff_one * right_side + coeff_two * image
    residual = right_side - coeff_one * image - coeff_two * second
    return (solution_field, residual)


def solution(mesh):
    finer = Mesh(
        mesh.devices.reshape(12, 2, 8, 2, 2), ("circ_0", "circ_1", "radax_0", "radax_1", "radax_2")
    )
    in_specs = (P(CIRC, RADAX), P(CIRC, RADAX), P(CIRC, RADAX), P(CIRC), P(CIRC))
    out_specs = (P(CIRC, RADAX), P(CIRC, RADAX))
    return jax.shard_map(local, mesh=finer, in_specs=in_specs, out_specs=out_specs, check_vma=False)
```

profile of v0, /device:TPU:1, one launch (start us, length us, event | category | flops | bytes accessed | tf_op | source)
XLA Modules:
  0.0 212.8 jit_solution(6143761249420690873)
XLA Ops:
  0.6 0.0 copy-start
  0.6 1.0 slice.110
  1.7 15.1 %collective-permute-start.2 = (f32[259,256]{1,0:T(8,128)S(1)}, f32[259,256]{1,0:T(8,128)S(1)}, u32[]{:S(2)}, u32[]{:S(2)}) collective-permute-start(f32[259,256]{1,0:T(8,128)S(1)} %slice.110), channel_id=1, source_target_pairs={{64,0},{96,32},{128,64},{160,96},{192,128},{224,160},{256,192},{28... | collective-permute-start | bytes 795656 | tf_op jit(solution)/shard_map/ppermute | solution.py:34
  16.8 0.0 copy-done
  16.8 4.6 %collective-permute-start.3 = (f32[260,256]{1,0:T(8,128)S(1)}, f32[260,256]{1,0:T(8,128)S(1)}, u32[]{:S(2)}, u32[]{:S(2)}) collective-permute-start(f32[260,256]{1,0:T(8,128)S(1)} %slice.111), channel_id=1, source_target_pairs={{96,0},{128,32},{160,64},{192,96},{224,128},{256,160},{288,192},{3... | collective-permute-start | bytes 798728 | tf_op jit(solution)/shard_map/ppermute | solution.py:34
  21.5 0.0 copy-start.5
  21.5 0.7 copy-done.5
  22.2 0.7 copy-done.4
  22.9 0.0 collective-permute-done.2
  22.9 6.6 %collective-permute-done.3 = f32[260,256]{1,0:T(8,128)S(1)} collective-permute-done((f32[260,256]{1,0:T(8,128)S(1)}, f32[260,256]{1,0:T(8,128)S(1)}, u32[]{:S(2)}, u32[]{:S(2)}) %collective-permute-start.3) | collective-permute-done | bytes 266272 | tf_op jit(solution)/shard_map/ppermute | solution.py:34
  29.6 1.6 gather_fusion
  31.1 1.6 gather_fusion.1
  32.7 0.2 multiply_add_fusion.2
  32.9 5.8 %collective-permute-start.4 = (f32[1,256]{1,0:T(1,128)S(1)}, f32[1,256]{1,0:T(1,128)S(1)}, u32[]{:S(2)}, u32[]{:S(2)}) collective-permute-start(f32[1,256]{1,0:T(1,128)S(1)} %get-tuple-element.39), channel_id=1, source_target_pairs={{0,32},{32,64},{64,96},{96,128},{128,160},{160,192},{192,224},{224... | collective-permute-start | bytes 3080 | tf_op jit(solution)/shard_map/ppermute | solution.py:22
  38.7 0.0 copy-start.1
  38.7 7.8 %collective-permute-start.5 = (f32[1,256]{1,0:T(1,128)S(1)}, f32[1,256]{1,0:T(1,128)S(1)}, u32[]{:S(2)}, u32[]{:S(2)}) collective-permute-start(f32[1,256]{1,0:T(1,128)S(1)} %get-tuple-element.40), channel_id=1, source_target_pairs={{32,0},{64,32},{96,64},{128,96},{160,128},{192,160},{224,192},{256... | collective-permute-start | bytes 3080 | tf_op jit(solution)/shard_map/ppermute | solution.py:24
  46.6 0.2 fusion.27
  46.8 0.0 collective-permute-done.4
  46.8 0.5 collective-permute-done.5
  47.3 0.3 fusion.10
  47.6 3.5 %scatter_custom_fusion = f32[519,256]{1,0:T(8,128)S(1)} fusion(s32[512]{0:T(512)S(1)} %get-tuple-element.44, f32[512,256]{1,0:T(8,128)S(1)} %fusion.10, f32[]{:T(128)} %constant.15.clone.1, f32[512]{0:T(512)S(1)} %copy-done.4), kind=kCustom, calls=%fused_computation.72 | custom fusion | flops 262144 | bytes 1057796 | tf_op jit(solution)/shard_map/scatter-add | solution.py:82
  51.2 3.6 %scatter_custom_fusion.1 = f32[519,256]{1,0:T(8,128)S(1)} fusion(f32[519,256]{1,0:T(8,128)S(1)} %scatter_custom_fusion, s32[512]{0:T(512)S(1)} %get-tuple-element.43, f32[512,256]{1,0:T(8,128)S(1)} %fusion.10, f32[512]{0:T(512)S(1)} %broadcast_subtract_fusion), kind=kCustom, calls=%fused_computation.70 | custom fusion | flops 262144 | bytes 1057792 | tf_op jit(solution)/shard_map/scatter-add | solution.py:83
  54.8 0.0 copy-start.2
  54.9 2.1 collective-permute-start.7
  56.9 1.9 collective-permute-start.6
  58.9 3.2 %collective-permute-start = (f32[1,256]{1,0:T(1,128)S(1)}, f32[1,256]{1,0:T(1,128)S(1)}, u32[]{:S(2)}, u32[]{:S(2)}) collective-permute-start(f32[1,256]{1,0:T(1,128)S(1)} %get-tuple-element.41), channel_id=1, source_target_pairs={{0,32},{32,64},{64,96},{96,128},{128,160},{160,192},{192,224},{224... | collective-permute-start | bytes 3080 | tf_op jit(solution)/shard_map/ppermute | solution.py:22
  62.0 6.0 %collective-permute-start.1 = (f32[1,256]{1,0:T(1,128)S(1)}, f32[1,256]{1,0:T(1,128)S(1)}, u32[]{:S(2)}, u32[]{:S(2)}) collective-permute-start(f32[1,256]{1,0:T(1,128)S(1)} %get-tuple-element.42), channel_id=1, source_target_pairs={{32,0},{64,32},{96,64},{128,96},{160,128},{192,160},{224,192},{256... | collective-permute-start | bytes 3080 | tf_op jit(solution)/shard_map/ppermute | solution.py:24
  68.0 11.6 %collective-permute-done = f32[1,256]{1,0:T(1,128)S(1)} collective-permute-done((f32[1,256]{1,0:T(1,128)S(1)}, f32[1,256]{1,0:T(1,128)S(1)}, u32[]{:S(2)}, u32[]{:S(2)}) %collective-permute-start) | collective-permute-done | bytes 1056 | tf_op jit(solution)/shard_map/ppermute | solution.py:22
  79.7 0.0 collective-permute-done.1
  79.7 0.0 collective-permute-done.6
  79.7 0.0 collective-permute-done.7
  79.7 0.4 fusion.5
  80.1 1.9 collective-permute-start.11
  82.1 1.9 collective-permute-start.10
  84.0 15.7 %collective-permute-done.10 = f32[259,256]{1,0:T(8,128)S(1)} collective-permute-done((f32[259,256]{1,0:T(8,128)S(1)}, f32[259,256]{1,0:T(8,128)S(1)}, u32[]{:S(2)}, u32[]{:S(2)}) %collective-permute-start.10) | collective-permute-done | bytes 265248 | tf_op jit(solution)/shard_map/ppermute | solution.py:34
  99.7 0.0 collective-permute-done.11
  99.7 1.6 gather_fusion.2
  101.3 1.6 gather_fusion.3
  102.9 0.2 multiply_add_fusion.1
  103.1 1.9 collective-permute-start.12
  105.1 7.2 %collective-permute-start.13 = (f32[1,256]{1,0:T(1,128)S(1)}, f32[1,256]{1,0:T(1,128)S(1)}, u32[]{:S(2)}, u32[]{:S(2)}) collective-permute-start(f32[1,256]{1,0:T(1,128)S(1)} %get-tuple-element.38), channel_id=1, source_target_pairs={{32,0},{64,32},{96,64},{128,96},{160,128},{192,160},{224,192},{256... | collective-permute-start | bytes 3080 | tf_op jit(solution)/shard_map/ppermute | solution.py:24
  112.2 0.2 fusion.26
  112.4 0.0 collective-permute-done.12
  112.4 0.3 collective-permute-done.13
  112.7 0.3 fusion.21
  113.1 3.5 %scatter_custom_fusion.2 = f32[519,256]{1,0:T(8,128)S(1)} fusion(s32[512]{0:T(512)S(1)} %get-tuple-element.44, f32[512,256]{1,0:T(8,128)S(1)} %fusion.21, f32[]{:T(128)} %constant.15.clone.1, f32[512]{0:T(512)S(1)} %copy-done.4), kind=kCustom, calls=%fused_computation.67 | custom fusion | flops 262144 | bytes 1057796 | tf_op jit(solution)/shard_map/scatter-add | solution.py:82
  116.6 3.6 %scatter_custom_fusion.3 = f32[519,256]{1,0:T(8,128)S(1)} fusion(f32[519,256]{1,0:T(8,128)S(1)} %scatter_custom_fusion.2, s32[512]{0:T(512)S(1)} %get-tuple-element.43, f32[512,256]{1,0:T(8,128)S(1)} %fusion.21, f32[512]{0:T(512)S(1)} %broadcast_subtract_fusion), kind=kCustom, calls=%fused_computation.65 | custom fusion | flops 262144 | bytes 1057792 | tf_op jit(solution)/shard_map/scatter-add | solution.py:83
  120.3 0.0 copy-start.3
  120.3 2.1 collective-permute-start.15
  122.4 1.9 collective-permute-start.14
  124.3 2.9 %collective-permute-start.8 = (f32[1,256]{1,0:T(1,128)S(1)}, f32[1,256]{1,0:T(1,128)S(1)}, u32[]{:S(2)}, u32[]{:S(2)}) collective-permute-start(f32[1,256]{1,0:T(1,128)S(1)} %get-tuple-element.35), channel_id=1, source_target_pairs={{0,32},{32,64},{64,96},{96,128},{128,160},{160,192},{192,224},{224... | collective-permute-start | bytes 3080 | tf_op jit(solution)/shard_map/ppermute | solution.py:22
  127.2 6.3 %collective-permute-start.9 = (f32[1,256]{1,0:T(1,128)S(1)}, f32[1,256]{1,0:T(1,128)S(1)}, u32[]{:S(2)}, u32[]{:S(2)}) collective-permute-start(f32[1,256]{1,0:T(1,128)S(1)} %get-tuple-element.36), channel_id=1, source_target_pairs={{32,0},{64,32},{96,64},{128,96},{160,128},{192,160},{224,192},{256... | collective-permute-start | bytes 3080 | tf_op jit(solution)/shard_map/ppermute | solution.py:24
  133.5 11.1 %collective-permute-done.8 = f32[1,256]{1,0:T(1,128)S(1)} collective-permute-done((f32[1,256]{1,0:T(1,128)S(1)}, f32[1,256]{1,0:T(1,128)S(1)}, u32[]{:S(2)}, u32[]{:S(2)}) %collective-permute-start.8) | collective-permute-done | bytes 1056 | tf_op jit(solution)/shard_map/ppermute | solution.py:22
  144.6 0.0 collective-permute-done.9
  144.6 0.0 collective-permute-done.14
  144.7 0.0 collective-permute-done.15
  144.7 0.0 copy-done.3
  144.7 1.1 multiply_reduce_fusion.4
  145.8 16.8 %all-reduce.8 = (f32[]{:T(128)}, f32[]{:T(128)}, f32[]{:T(128)}, f32[]{:T(128)}, f32[]{:T(128)}) all-reduce(f32[]{:T(128)} %get-tuple-element.6, f32[]{:T(128)} %get-tuple-element.3, f32[]{:T(128)} %get-tuple-element.5, f32[]{:T(128)} %get-tuple-element.4, ...), channel_id=1, replica_groups=mesh['circ_0'=12,'circ_1'=2,'radax_0'=8,'radax_1'=2,'radax_2'=2] {'circ_0'}, use_global_device_ids=true, to_apply=%region_29.30 | all-reduce | flops 5 | bytes 40 | tf_op jit(solution)/shard_map/psum | solution.py:39
  162.6 6.0 %all-reduce.12 = (f32[]{:T(128)}, f32[]{:T(128)}, f32[]{:T(128)}, f32[]{:T(128)}, f32[]{:T(128)}) all-reduce(f32[]{:T(128)} %get-tuple-element.7, f32[]{:T(128)} %get-tuple-element.8, f32[]{:T(128)} %get-tuple-element.9, ...), channel_id=1, replica_groups=mesh['circ_0'=12,'circ_1'=2,'radax_0'=8,'radax_1'=2,'radax_2'=2] {'circ_1'}, use_global_device_ids=true, to_apply=%region_30.31 | all-reduce | flops 5 | bytes 40 | tf_op jit(solution)/shard_map/psum | solution.py:39
  168.6 14.6 %all-reduce.9 = (f32[]{:T(128)}, f32[]{:T(128)}, f32[]{:T(128)}, f32[]{:T(128)}, f32[]{:T(128)}) all-reduce(f32[]{:T(128)} %get-tuple-element.27, f32[]{:T(128)} %get-tuple-element.28, f32[]{:T(128)} %get-tuple-element.29, ...), channel_id=1, replica_groups=mesh['circ_0'=12,'circ_1'=2,'radax_0'=8,'radax_1'=2,'radax_2'=2] {'radax..., use_global_device_ids=true, to_apply=%region_31.32 | all-reduce | flops 5 | bytes 40 | tf_op jit(solution)/shard_map/psum | solution.py:39
  183.1 4.5 %all-reduce.11 = (f32[]{:T(128)}, f32[]{:T(128)}, f32[]{:T(128)}, f32[]{:T(128)}, f32[]{:T(128)}) all-reduce(f32[]{:T(128)} %get-tuple-element.12, f32[]{:T(128)} %get-tuple-element.13, f32[]{:T(128)} %get-tuple-element.14, ...), channel_id=1, replica_groups=mesh['circ_0'=12,'circ_1'=2,'radax_0'=8,'radax_1'=2,'radax_2'=2] {'radax..., use_global_device_ids=true, to_apply=%region_32.33 | all-reduce | flops 5 | bytes 40 | tf_op jit(solution)/shard_map/psum | solution.py:39
  187.7 16.5 %all-reduce.10 = (f32[]{:T(128)}, f32[]{:T(128)}, f32[]{:T(128)}, f32[]{:T(128)}, f32[]{:T(128)}) all-reduce(f32[]{:T(128)} %get-tuple-element.22, f32[]{:T(128)} %get-tuple-element.23, f32[]{:T(128)} %get-tuple-element.24, ...), channel_id=1, replica_groups=mesh['circ_0'=12,'circ_1'=2,'radax_0'=8,'radax_1'=2,'radax_2'=2] {'radax..., use_global_device_ids=true, to_apply=%region_33.34 | all-reduce | flops 5 | bytes 40 | tf_op jit(solution)/shard_map/psum | solution.py:39
  211.7 1.1 multiply_subtract_fusion
  (19 shorter events, 0.3 us)
Async XLA Ops:
  0.6 16.2 %copy-start = (f32[512,256]{1,0:T(8,128)S(1)}, f32[512,256]{1,0:T(8,128)}, u32[]{:S(2)}) copy-start(f32[512,256]{1,0:T(8,128)} %param.5) | copy-start | bytes 1572868
  1.7 21.2 %collective-permute-start.2 = (f32[259,256]{1,0:T(8,128)S(1)}, f32[259,256]{1,0:T(8,128)S(1)}, u32[]{:S(2)}, u32[]{:S(2)}) collective-permute-start(f32[259,256]{1,0:T(8,128)S(1)} %slice.110), channel_id=1, source_target_pairs={{64,0},{96,32},{128,64},{160,96},{192,128},{224,160},{256,192},{28... | collective-permute-start | bytes 795656 | tf_op jit(solution)/shard_map/ppermute | solution.py:34
  16.8 12.7 %collective-permute-start.3 = (f32[260,256]{1,0:T(8,128)S(1)}, f32[260,256]{1,0:T(8,128)S(1)}, u32[]{:S(2)}, u32[]{:S(2)}) collective-permute-start(f32[260,256]{1,0:T(8,128)S(1)} %slice.111), channel_id=1, source_target_pairs={{96,0},{128,32},{160,64},{192,96},{224,128},{256,160},{288,192},{3... | collective-permute-start | bytes 798728 | tf_op jit(solution)/shard_map/ppermute | solution.py:34
  21.5 0.7 copy-start.5
  22.2 0.7 copy-start.4
  32.9 13.9 %collective-permute-start.4 = (f32[1,256]{1,0:T(1,128)S(1)}, f32[1,256]{1,0:T(1,128)S(1)}, u32[]{:S(2)}, u32[]{:S(2)}) collective-permute-start(f32[1,256]{1,0:T(1,128)S(1)} %get-tuple-element.39), channel_id=1, source_target_pairs={{0,32},{32,64},{64,96},{96,128},{128,160},{160,192},{192,224},{224... | collective-permute-start | bytes 3080 | tf_op jit(solution)/shard_map/ppermute | solution.py:22
  38.7 8.5 %copy-start.1 = (f32[512,256]{1,0:T(8,128)S(1)}, f32[512,256]{1,0:T(8,128)}, u32[]{:S(2)}) copy-start(f32[512,256]{1,0:T(8,128)} %param.7) | copy-start | bytes 1572868
  38.7 8.5 %collective-permute-start.5 = (f32[1,256]{1,0:T(1,128)S(1)}, f32[1,256]{1,0:T(1,128)S(1)}, u32[]{:S(2)}, u32[]{:S(2)}) collective-permute-start(f32[1,256]{1,0:T(1,128)S(1)} %get-tuple-element.40), channel_id=1, source_target_pairs={{32,0},{64,32},{96,64},{128,96},{160,128},{192,160},{224,192},{256... | collective-permute-start | bytes 3080 | tf_op jit(solution)/shard_map/ppermute | solution.py:24
  54.8 24.9 %copy-start.2 = (f32[512,256]{1,0:T(8,128)S(1)}, f32[512,256]{1,0:T(8,128)}, u32[]{:S(2)}) copy-start(f32[512,256]{1,0:T(8,128)} %param.6) | copy-start | bytes 1572868
  54.9 24.8 %collective-permute-start.7 = (f32[260,256]{1,0:T(8,128)S(1)}, f32[260,256]{1,0:T(8,128)S(1)}, u32[]{:S(2)}, u32[]{:S(2)}) collective-permute-start(f32[260,256]{1,0:T(8,128)S(1)} %slice.147), channel_id=1, source_target_pairs={{672,0},{704,32},{736,64},{0,96},{32,128},{64,160},{96,192},{128,2... | collective-permute-start | bytes 798728 | tf_op jit(solution)/shard_map/ppermute | solution.py:34
  56.9 22.7 %collective-permute-start.6 = (f32[259,256]{1,0:T(8,128)S(1)}, f32[259,256]{1,0:T(8,128)S(1)}, u32[]{:S(2)}, u32[]{:S(2)}) collective-permute-start(f32[259,256]{1,0:T(8,128)S(1)} %slice.146), channel_id=1, source_target_pairs={{704,0},{736,32},{0,64},{32,96},{64,128},{96,160},{128,192},{160,2... | collective-permute-start | bytes 795656 | tf_op jit(solution)/shard_map/ppermute | solution.py:34
  58.9 20.8 %collective-permute-start = (f32[1,256]{1,0:T(1,128)S(1)}, f32[1,256]{1,0:T(1,128)S(1)}, u32[]{:S(2)}, u32[]{:S(2)}) collective-permute-start(f32[1,256]{1,0:T(1,128)S(1)} %get-tuple-element.41), channel_id=1, source_target_pairs={{0,32},{32,64},{64,96},{96,128},{128,160},{160,192},{192,224},{224... | collective-permute-start | bytes 3080 | tf_op jit(solution)/shard_map/ppermute | solution.py:22
  62.0 17.6 %collective-permute-start.1 = (f32[1,256]{1,0:T(1,128)S(1)}, f32[1,256]{1,0:T(1,128)S(1)}, u32[]{:S(2)}, u32[]{:S(2)}) collective-permute-start(f32[1,256]{1,0:T(1,128)S(1)} %get-tuple-element.42), channel_id=1, source_target_pairs={{32,0},{64,32},{96,64},{128,96},{160,128},{192,160},{224,192},{256... | collective-permute-start | bytes 3080 | tf_op jit(solution)/shard_map/ppermute | solution.py:24
  80.1 19.6 %collective-permute-start.11 = (f32[260,256]{1,0:T(8,128)S(1)}, f32[260,256]{1,0:T(8,128)S(1)}, u32[]{:S(2)}, u32[]{:S(2)}) collective-permute-start(f32[260,256]{1,0:T(8,128)S(1)} %slice.151), channel_id=1, source_target_pairs={{96,0},{128,32},{160,64},{192,96},{224,128},{256,160},{288,192},{3... | collective-permute-start | bytes 798728 | tf_op jit(solution)/shard_map/ppermute | solution.py:34
  82.1 17.6 %collective-permute-start.10 = (f32[259,256]{1,0:T(8,128)S(1)}, f32[259,256]{1,0:T(8,128)S(1)}, u32[]{:S(2)}, u32[]{:S(2)}) collective-permute-start(f32[259,256]{1,0:T(8,128)S(1)} %slice.150), channel_id=1, source_target_pairs={{64,0},{96,32},{128,64},{160,96},{192,128},{224,160},{256,192},{28... | collective-permute-start | bytes 795656 | tf_op jit(solution)/shard_map/ppermute | solution.py:34
  103.1 9.3 %collective-permute-start.12 = (f32[1,256]{1,0:T(1,128)S(1)}, f32[1,256]{1,0:T(1,128)S(1)}, u32[]{:S(2)}, u32[]{:S(2)}) collective-permute-start(f32[1,256]{1,0:T(1,128)S(1)} %get-tuple-element.37), channel_id=1, source_target_pairs={{0,32},{32,64},{64,96},{96,128},{128,160},{160,192},{192,224},{224... | collective-permute-start | bytes 3080 | tf_op jit(solution)/shard_map/ppermute | solution.py:22
  105.1 7.7 %collective-permute-start.13 = (f32[1,256]{1,0:T(1,128)S(1)}, f32[1,256]{1,0:T(1,128)S(1)}, u32[]{:S(2)}, u32[]{:S(2)}) collective-permute-start(f32[1,256]{1,0:T(1,128)S(1)} %get-tuple-element.38), channel_id=1, source_target_pairs={{32,0},{64,32},{96,64},{128,96},{160,128},{192,160},{224,192},{256... | collective-permute-start | bytes 3080 | tf_op jit(solution)/shard_map/ppermute | solution.py:24
  120.3 24.4 %copy-start.3 = (f32[512,256]{1,0:T(8,128)S(1)}, f32[512,256]{1,0:T(8,128)}, u32[]{:S(2)}) copy-start(f32[512,256]{1,0:T(8,128)} %param.6) | copy-start | bytes 1572868
  120.3 24.3 %collective-permute-start.15 = (f32[260,256]{1,0:T(8,128)S(1)}, f32[260,256]{1,0:T(8,128)S(1)}, u32[]{:S(2)}, u32[]{:S(2)}) collective-permute-start(f32[260,256]{1,0:T(8,128)S(1)} %slice.155), channel_id=1, source_target_pairs={{672,0},{704,32},{736,64},{0,96},{32,128},{64,160},{96,192},{128,2... | collective-permute-start | bytes 798728 | tf_op jit(solution)/shard_map/ppermute | solution.py:34
  122.4 22.3 %collective-permute-start.14 = (f32[259,256]{1,0:T(8,128)S(1)}, f32[259,256]{1,0:T(8,128)S(1)}, u32[]{:S(2)}, u32[]{:S(2)}) collective-permute-start(f32[259,256]{1,0:T(8,128)S(1)} %slice.154), channel_id=1, source_target_pairs={{704,0},{736,32},{0,64},{32,96},{64,128},{96,160},{128,192},{160,2... | collective-permute-start | bytes 795656 | tf_op jit(solution)/shard_map/ppermute | solution.py:34
  124.3 20.3 %collective-permute-start.8 = (f32[1,256]{1,0:T(1,128)S(1)}, f32[1,256]{1,0:T(1,128)S(1)}, u32[]{:S(2)}, u32[]{:S(2)}) collective-permute-start(f32[1,256]{1,0:T(1,128)S(1)} %get-tuple-element.35), channel_id=1, source_target_pairs={{0,32},{32,64},{64,96},{96,128},{128,160},{160,192},{192,224},{224... | collective-permute-start | bytes 3080 | tf_op jit(solution)/shard_map/ppermute | solution.py:22
  127.2 17.4 %collective-permute-start.9 = (f32[1,256]{1,0:T(1,128)S(1)}, f32[1,256]{1,0:T(1,128)S(1)}, u32[]{:S(2)}, u32[]{:S(2)}) collective-permute-start(f32[1,256]{1,0:T(1,128)S(1)} %get-tuple-element.36), channel_id=1, source_target_pairs={{32,0},{64,32},{96,64},{128,96},{160,128},{192,160},{224,192},{256... | collective-permute-start | bytes 3080 | tf_op jit(solution)/shard_map/ppermute | solution.py:24
where the time goes:
time: 214 us; the launch traced here: 213 us
  starting transfers between devices  72.5 us (34%)
  blocking collectives  58.4 us (27%)
  waiting for transfers between devices  45.9 us (21%)
  other arithmetic  18.6 us (9%)
  local copies, waits for them, and re-layouts  8.85 us (4%)
  between operations  8.63 us (4%)
    psum x5, blocking collectives, over_axes(): shard = lax.psum(shard, axis)  58.4 us
    ppermute x8, starting transfers between devices, shifted(): return lax.ppermute(block, axis, route)  31.5 us
    ppermute x4, starting transfers between devices, with_halo(): lax.ppermute(head, axis, [((i + 1) % count, i) for i in range(count)])  27.2 us
    ppermute x4, waiting for transfers between devices, with_halo(): lax.ppermute(tail, axis, [(i, (i + 1) % count) for i in range(count)])  22.8 us
    ppermute x8, waiting for transfers between devices, shifted(): return lax.ppermute(block, axis, route)  22.3 us
    ppermute x4, starting transfers between devices, with_halo(): lax.ppermute(tail, axis, [(i, (i + 1) % count) for i in range(count)])  13.8 us
    scatter-add x2, other arithmetic, give_back(): collect = collect.at[after_idx].add((1.0 - weight) * response)  7.24 us
    scatter-add x2, other arithmetic, give_back(): collect = collect.at[local_idx].add(weight * response)  7.09 us
  transfers between devices with their start and end apart: 16, of which 6 were waited for; matrix products, arithmetic and copies ran while one was open for 0% of the time, Pallas kernels for 0%

commit v1 on v0

v1 whole, which is shorter than its diff:
```python
import jax
import jax.numpy as jnp
from jax import lax
from jax.experimental import pallas as pl
from jax.experimental.pallas import tpu as pltpu
from jax.sharding import Mesh
from jax.sharding import PartitionSpec as P

AXES = ("z", "xh", "y", "xl", "core")
SIZES = (12, 2, 8, 2, 2)
CIRC = 24
ROWS = 512
W = 256
NROWS = CIRC * ROWS
PAD = 8
EXT = 544
MESH = pl.DeviceIdType.MESH
HIGH = lax.Precision.HIGHEST

CHUNKS = (
    [(0, 16, 0, 24)]
    + [(16 + 128 * k, 128, 8 + 128 * k, 144) for k in range(4)]
    + [(528, 16, 520, 24)]
)
X_PARTNERS = [(0, a, 0, b, k) for a in range(2) for b in range(2) for k in range(2) if a + b + k]
Y_PARTNERS = [(0, 0, d, 0, 0) for d in range(1, 8)]
Z_PARTNERS = [(d, 0, 0, 0, 0) for d in range(1, 12)]
EXTRA = [(d, 1, 0, 0, 0) for d in (1, 2, 10, 11)]


def kernel(r_in, cr_in, cs_in, m_in, w_in, image_out, second_out, y_out,
           u, cr, cs, v, im, se, m3, m2, w3, w2, pt_big, p_big, pt_small, p_small,
           mine, from_x, from_y, from_z, local_sem, send_sem, recv_sem, ar_send, ar_recv, out_sem):
    me = [lax.axis_index(a) for a in AXES]
    circ = me[0] * 2 + me[1]

    def along(shift):
        c = lax.rem(circ + (shift + CIRC), CIRC)
        return (lax.div(c, 2), lax.rem(c, 2), me[2], me[3], me[4])

    def at(offset):
        return tuple(lax.rem(p + o, n) if o else p for p, o, n in zip(me, offset, SIZES))

    barrier = pltpu.get_barrier_semaphore()
    greeted = X_PARTNERS + Y_PARTNERS + Z_PARTNERS + EXTRA
    for offset in greeted:
        pl.semaphore_signal(barrier, inc=1, device_id=at(offset), device_id_type=MESH)
    own = [
        pltpu.make_async_copy(r_in, u.at[pl.ds(PAD + 16, ROWS)], local_sem.at[0]),
        pltpu.make_async_copy(cr_in, cr.at[pl.ds(PAD + 16, ROWS)], local_sem.at[1]),
    ]
    for copy in own:
        copy.start()
    nothing = jnp.zeros((PAD, W), jnp.float32)
    for ref in (u, v):
        ref[0:PAD] = nothing
        ref[PAD + EXT : PAD + EXT + PAD] = nothing
    for ref in (im, se):
        ref[...] = jnp.zeros(ref.shape, jnp.float32)
    pl.semaphore_wait(barrier, len(greeted))

    def send(i, src, dst, shift):
        return pltpu.make_async_remote_copy(
            src_ref=src, dst_ref=dst, send_sem=send_sem.at[i], recv_sem=recv_sem.at[i],
            device_id=along(shift), device_id_type=MESH)

    small = [
        send(0, m_in, m3, 3), send(1, w_in, w3, 3), send(2, m_in, m2, 2), send(3, w_in, w2, 2),
        send(4, r_in.at[pl.ds(0, 16)], u.at[pl.ds(PAD + 528, 16)], -1),
        send(5, r_in.at[pl.ds(496, 16)], u.at[pl.ds(PAD, 16)], 1),
        send(6, cr_in.at[pl.ds(0, 8)], cr.at[pl.ds(PAD + 528, 8)], -1),
        send(7, cr_in.at[pl.ds(504, 8)], cr.at[pl.ds(PAD + 8, 8)], 1),
    ]
    bulk = [
        send(8, cs_in.at[pl.ds(240, 144)], cs.at[pl.ds(PAD + 0, 144)], 3),
        send(9, cs_in.at[pl.ds(384, 128)], cs.at[pl.ds(PAD + 144, 128)], 3),
        send(10, cs_in.at[pl.ds(0, 128)], cs.at[pl.ds(PAD + 272, 128)], 2),
        send(11, cs_in.at[pl.ds(128, 144)], cs.at[pl.ds(PAD + 400, 144)], 2),
    ]
    for copy in small + bulk:
        copy.start()

    col = lax.broadcasted_iota(jnp.int32, (1, W), 1)
    not_first = col > 0
    not_last = col < W - 1

    def around(ref, start, count):
        mid = ref[pl.ds(start, count)]
        beside = (jnp.where(not_first, pltpu.roll(mid, 1, 1), 0.0)
                  + jnp.where(not_last, pltpu.roll(mid, W - 1, 1), 0.0))
        return mid, 0.25 * (ref[pl.ds(start - 1, count)] + ref[pl.ds(start + 1, count)] + beside)

    for copy in small[:4]:
        copy.wait()
    base = circ * ROWS - 16
    eye = jnp.where(lax.broadcasted_iota(jnp.int32, (128, 128), 0)
                    == lax.broadcasted_iota(jnp.int32, (128, 128), 1), 1.0, 0.0).astype(jnp.float32)

    def mortar(rows, weights, first, count, lanes):
        place = rows - base
        place = jnp.where(place < 0, place + NROWS, place)
        place = jnp.where(place >= NROWS, place - NROWS, place)
        line = lax.broadcasted_iota(jnp.int32, (count, lanes), 0) + first
        return jnp.where(line == place, weights, 0.0) + jnp.where(line == place + 1, 1.0 - weights, 0.0)

    def lanes16(row, roll):
        return (pltpu.roll(row, roll, 1) if roll else row)[:, :16]

    sources = [(m3, w3, 2), (m3, w3, 3), (m2, w2, 0), (m2, w2, 1)]
    for k, (m, w, line) in enumerate(sources):
        pt = mortar(m[line : line + 1, :], w[line : line + 1, :], 8 + 128 * k, 144, 128)
        pt_big[k] = pt
        p_big[k] = lax.dot_general(eye, pt, (((1,), (1,)), ((), ())), precision=HIGH,
                                   preferred_element_type=jnp.float32)
    for k, (m, w, line, roll, first) in enumerate([(m3, w3, 1, 16, 0), (m2, w2, 2, 0, 520)]):
        pt = mortar(lanes16(m[line : line + 1, :], roll), lanes16(w[line : line + 1, :], roll), first, 24, 16)
        pt_small[k] = pt
        p_small[k] = lax.dot_general(eye[:16, :16], pt, (((1,), (1,)), ((), ())), precision=HIGH,
                                     preferred_element_type=jnp.float32)

    def matrices(i):
        if i == 0 or i == 5:
            return p_small[i // 5], pt_small[i // 5]
        return p_big[i - 1], pt_big[i - 1]

    def project(ref):
        for i, (first, count, rotor, rotor_count) in enumerate(CHUNKS):
            v[pl.ds(PAD + first, count)] = jnp.dot(
                matrices(i)[0], ref[pl.ds(PAD + rotor, rotor_count)], precision=HIGH,
                preferred_element_type=jnp.float32)

    def give_back(ref, i):
        first, count, rotor, rotor_count = CHUNKS[i]
        mid, rest = around(v, PAD + first, count)
        response = cs[pl.ds(PAD + first, count)] * mid - rest
        ref[pl.ds(PAD + rotor, rotor_count)] += jnp.dot(
            matrices(i)[1], response, precision=HIGH, preferred_element_type=jnp.float32)

    def rotor_part(ref, out, start, count):
        mid, rest = around(ref, start, count)
        out[pl.ds(start, count)] = cr[pl.ds(start, count)] * mid - rest

    for copy in own:
        copy.wait()
    for copy in small[4:]:
        copy.wait()
    project(u)
    for q in range(4):
        rotor_part(u, im, PAD + 8 + 132 * q + 4 * (q % 2), 136 if q % 2 == 0 else 128)
    bulk[0].wait()
    give_back(im, 0)
    give_back(im, 1)
    bulk[1].wait()
    give_back(im, 2)
    bulk[2].wait()
    give_back(im, 3)
    bulk[3].wait()
    give_back(im, 4)
    give_back(im, 5)
    image_copy = pltpu.make_async_copy(im.at[pl.ds(PAD + 16, ROWS)], image_out, out_sem.at[0])
    project(im)
    for q in range(4):
        rotor_part(im, se, PAD + 16 + 128 * q, 128)
    for i in range(6):
        give_back(se, i)
    image_copy.start()
    second_copy = pltpu.make_async_copy(se.at[pl.ds(PAD + 16, ROWS)], second_out, out_sem.at[1])

    parts = [jnp.zeros((8, W), jnp.float32)] * 5
    for q in range(8):
        at_rows = pl.ds(PAD + 16 + 64 * q, 64)
        b, p, s = u[at_rows], im[at_rows], se[at_rows]
        for n, product in enumerate((b * p, b * s, p * p, p * s, s * s)):
            parts[n] = parts[n] + jnp.sum(product.reshape(8, 8, W), axis=0)
    lane = lax.broadcasted_iota(jnp.int32, (1, 128), 1)
    total = jnp.zeros((1, 128), jnp.float32)
    for n, part in enumerate(parts):
        total = jnp.where(lane == n, jnp.sum(part), total)
    second_copy.start()

    done = 0
    for stage, (partners, got) in enumerate(((X_PARTNERS, from_x), (Y_PARTNERS, from_y), (Z_PARTNERS, from_z))):
        mine[stage] = total
        copies = [
            pltpu.make_async_remote_copy(
                src_ref=mine.at[stage], dst_ref=got.at[pl.ds(n, 1)],
                send_sem=ar_send.at[done + n], recv_sem=ar_recv.at[done + n],
                device_id=at(offset), device_id_type=MESH)
            for n, offset in enumerate(partners)
        ]
        done += len(partners)
        for copy in copies:
            copy.start()
        for copy in copies:
            copy.wait()
        total = total + jnp.sum(got[0 : len(partners)], axis=0, keepdims=True)

    def pick(n):
        return jnp.sum(jnp.where(lane == n, total, 0.0), axis=1, keepdims=True)

    cross_one, cross_two, gram_pp, gram_pq, gram_qq = [pick(n) for n in range(5)]
    determinant = gram_pp * gram_qq - gram_pq * gram_pq
    y1 = (gram_qq * cross_one - gram_pq * cross_two) / determinant
    y2 = (gram_pp * cross_two - gram_pq * cross_one) / determinant
    y_out[0:8] = jnp.broadcast_to(y1, (8, W))
    y_out[8:16] = jnp.broadcast_to(y2, (8, W))
    image_copy.wait()
    second_copy.wait()


def local(right_side, coef_rotor, coef_stator, mortar_rows, mortar_weight):
    f32 = jnp.float32
    block = jax.ShapeDtypeStruct((ROWS, W), f32)
    wide = pltpu.VMEM((PAD + EXT + PAD, W), f32)
    hbm = pl.BlockSpec(memory_space=pl.ANY)
    image, second, y = pl.pallas_call(
        kernel,
        out_shape=(block, block, jax.ShapeDtypeStruct((16, W), f32)),
        in_specs=[hbm] * 5,
        out_specs=(hbm, hbm, pl.BlockSpec(memory_space=pltpu.VMEM)),
        scratch_shapes=[wide] * 6
        + [pltpu.VMEM((4, 128), jnp.int32)] * 2
        + [pltpu.VMEM((4, 128), f32)] * 2
        + [
            pltpu.VMEM((4, 144, 128), f32),
            pltpu.VMEM((4, 128, 144), f32),
            pltpu.VMEM((2, 24, 16), f32),
            pltpu.VMEM((2, 16, 24), f32),
            pltpu.VMEM((3, 1, 128), f32),
            pltpu.VMEM((8, 128), f32),
            pltpu.VMEM((8, 128), f32),
            pltpu.VMEM((16, 128), f32),
            pltpu.SemaphoreType.DMA((2,)),
            pltpu.SemaphoreType.DMA((12,)),
            pltpu.SemaphoreType.DMA((12,)),
            pltpu.SemaphoreType.DMA((25,)),
            pltpu.SemaphoreType.DMA((25,)),
            pltpu.SemaphoreType.DMA((2,)),
        ],
        compiler_params=pltpu.CompilerParams(collective_id=0, has_side_effects=True),
    )(right_side, coef_rotor, coef_stator, mortar_rows.reshape(4, 128), mortar_weight.reshape(4, 128))
    y1, y2 = y[0:1], y[8:9]
    return y1 * right_side + y2 * image, right_side - y1 * image - y2 * second


def solution(mesh):
    finer = Mesh(mesh.devices.reshape(SIZES), AXES)
    circ, radax = AXES[:2], AXES[2:]
    whole = P(circ, radax)
    return jax.shard_map(local, mesh=finer, in_specs=(whole, whole, whole, P(circ), P(circ)),
                         out_specs=(whole, whole), check_vma=False)
```

time: 214 us -> 61.2 us (0.29)
  starting transfers between devices: 72.5 us -> 0 us
  blocking collectives: 58.4 us -> 0 us
  Pallas kernels: 0 us -> 57.2 us
  waiting for transfers between devices: 45.9 us -> 0 us
  other arithmetic: 18.6 us -> 2.29 us
  local copies, waits for them, and re-layouts: 8.85 us -> 0.72 us
  between operations: 8.63 us -> 0.65 us
    ppermute x16 -> x0, starting transfers between devices: 72.5 us -> none  [the longest x8 31.5 us: shifted(): return lax.ppermute(block, axis, route)]
    psum x5 -> x0, blocking collectives: 58.4 us -> none  [over_axes(): shard = lax.psum(shard, axis)]
    pallas_call x0 -> x1, Pallas kernels: none -> 57.2 us  [local(): pl.pallas_call(kernel, out_shape=(block, block, jax.ShapeDtypeStruct((16,...]
    ppermute x16 -> x0, waiting for transfers between devices: 45.9 us -> none  [the longest x4 22.8 us: with_halo(): lax.ppermute(tail, axis, [(i, (i + 1) % count) for i in range(count)])]
    scatter-add x4 -> x0, other arithmetic: 14.3 us -> none  [the longest x2 7.24 us: give_back(): collect = collect.at[after_idx].add((1.0 - weight) * response)]
    gather x4 -> x0, local copies, waits for them, and re-layouts: 6.29 us -> none  [project(): return weight * window[local_idx] + (1.0 - weight) * window[after_idx]]
  transfers between devices with their start and end apart: 16 -> 0, of which waited for: 6 -> 0; matrix products, arithmetic and copies ran while one was open for 0% -> 0% of each run, Pallas kernels for 0% -> 0%
where the time goes in v1:
time: 61.2 us; the launch traced here: 60.9 us
  Pallas kernels  57.2 us (93%)
  other arithmetic  2.29 us (4%)
  local copies, waits for them, and re-layouts  0.72 us (1%)
  between operations  0.65 us (1%)
    pallas_call x1, Pallas kernels, local(): pl.pallas_call(kernel, out_shape=(block, block, jax.ShapeDtypeStruct((16,...  57.2 us
    sub x1, other arithmetic, local(): return (y1 * right_side + y2 * image, right_side - y1 * image - y2 * second)  2.29 us

profile of v1, /device:TPU:1, one launch (start us, length us, event | category | flops | bytes accessed | tf_op | source)
XLA Modules:
  0.0 60.9 jit_solution(17992637938964515169)
XLA Ops:
  0.6 0.0 copy-start
  0.6 57.2 %shard_map.68 = (f32[512,256]{1,0:T(8,128)}, f32[512,256]{1,0:T(8,128)}, f32[16,256]{1,0:T(8,128)}) custom-call(f32[512,256]{1,0:T(8,128)} %r_in.1, f32[512,256]{1,0:T(8,128)} %cr_in.1, f32[512,256]{1,0:T(8,128)} %cs_in.1, s32[4,128]{1,0:T(4,128)} %bitcast.6, f32[4,128]{1,0:T(4,128)} %bitcast.7), custom_call_target="tpu_custom_call" | custom-call | tf_op jit(solution)/shard_map/pallas_call | solution.py:216
  57.9 0.7 %fusion = (f32[1,256]{1,0:T(1,128)S(1)}, f32[1,256]{1,0:T(1,128)S(1)}) fusion(f32[16,256]{1,0:T(8,128)} %get-tuple-element.5), kind=kLoop, calls=%fused_computation.2 | loop fusion | bytes 4096 | tf_op jit(solution)/shard_map/slice | solution.py:242
  58.6 0.0 copy-done
  58.6 2.3 %multiply_subtract_fusion = (f32[512,256]{1,0:T(8,128)}, f32[512,256]{1,0:T(8,128)}) fusion(f32[512,256]{1,0:T(8,128)} %get-tuple-element.7, f32[512,256]{1,0:T(8,128)S(1)} %copy-done, f32[512,256]{1,0:T(8,128)} %get-tuple-element.6, f32[256]{0:T(256)S(1)} %bitcast.5, f32[256]{0:T(256)S(1)} %bitcast.4), kind=kLoop, calls=%fused_computation | loop fusion | flops 917504 | bytes 2623488 | tf_op jit(solution)/shard_map/sub | solution.py:243
Async XLA Ops:
  0.6 58.0 %copy-start = (f32[512,256]{1,0:T(8,128)S(1)}, f32[512,256]{1,0:T(8,128)}, u32[]{:S(2)}) copy-start(f32[512,256]{1,0:T(8,128)} %r_in.1) | copy-start | bytes 1572868

commit v2 on v1

v2 whole, which is shorter than its diff:
```python
import jax
import jax.numpy as jnp
from jax import lax
from jax.experimental import pallas as pl
from jax.experimental.pallas import tpu as pltpu
from jax.sharding import Mesh
from jax.sharding import PartitionSpec as P

AXES = ("z", "xh", "y", "xl", "core")
SIZES = (12, 2, 8, 2, 2)
CIRC = 24
ROWS = 512
W = 256
NROWS = CIRC * ROWS
PAD = 8
EXT = 544
CUT = 272
HELP = 272
MESH = pl.DeviceIdType.MESH
HIGH = lax.Precision.HIGHEST
F32 = jnp.float32

FRONT = [(0, 16, 3, 1, 112), (16, 128, 3, 2, 0), (144, 128, 3, 3, 0), (272, 32, 2, 0, 0)]
BACK = [(304, 96, 2, 0, 32), (400, 128, 2, 1, 0), (528, 16, 2, 2, 0)]
OWN = [(0, 128, 0, 0, 0), (128, 128, 0, 1, 0), (256, 16, 0, 2, 0)]
X_PARTNERS = [(0, a, 0, b, k) for a in range(2) for b in range(2) for k in range(2) if a + b + k]
Y_PARTNERS = [(0, 0, d, 0, 0) for d in range(1, 8)]
Z_PARTNERS = [(d, 0, 0, 0, 0) for d in range(1, 12)]
NEAR = [(d, a, 0, 0, 0) for d in (1, 2, 10, 11) for a in range(2)]
N_SENDS = 16


def window(piece, size):
    low = max(piece[0] - 8, 0)
    return low, min(piece[0] + piece[1] + 8, size) - low


SHAPES = [(window(p, EXT)[1], p[1]) for p in FRONT + BACK] + [(window(p, HELP)[1], p[1]) for p in OWN]


def kernel(r_in, cr_in, cs_in, m_in, w_in, image_out, second_out, y1_out, y2_out,
           u, cr, cs, v, v2, im, se, se2, uh, crh, csh, vh, vh2, imh, seh,
           m3, m2, m0, w3, w2, w0, mine, from_x, from_y, from_z,
           local_sem, send_sem, recv_sem, ar_send, ar_recv, token, *matrices):
    me = [lax.axis_index(a) for a in AXES]
    circ = me[0] * 2 + me[1]
    count = len(SHAPES)
    give, take = matrices[:count], matrices[count:]

    def along(shift):
        c = lax.rem(circ + (shift + CIRC), CIRC)
        return (lax.div(c, 2), lax.rem(c, 2), me[2], me[3], me[4])

    def at(offset):
        return tuple(lax.rem(p + o, n) if o else p for p, o, n in zip(me, offset, SIZES))

    barrier = pltpu.get_barrier_semaphore()
    greeted = X_PARTNERS + Y_PARTNERS + NEAR
    for offset in greeted:
        pl.semaphore_signal(barrier, inc=1, device_id=at(offset), device_id_type=MESH)
    own = [
        pltpu.make_async_copy(m_in, m0, local_sem.at[0]),
        pltpu.make_async_copy(w_in, w0, local_sem.at[1]),
        pltpu.make_async_copy(r_in, u.at[pl.ds(PAD + 16, ROWS)], local_sem.at[2]),
        pltpu.make_async_copy(cr_in, cr.at[pl.ds(PAD + 16, ROWS)], local_sem.at[3]),
        pltpu.make_async_copy(cs_in.at[pl.ds(0, HELP)], csh.at[pl.ds(PAD, HELP)], local_sem.at[4]),
    ]
    for copy in own:
        copy.start()

    def send(i, src, dst, shift):
        return pltpu.make_async_remote_copy(
            src_ref=src, dst_ref=dst, send_sem=send_sem.at[i], recv_sem=recv_sem.at[i],
            device_id=along(shift), device_id_type=MESH)

    def rows(ref, first, n):
        return ref.at[pl.ds(first, n)]

    mortar_sends = [send(0, m_in, m3, 3), send(1, w_in, w3, 3), send(2, m_in, m2, 2), send(3, w_in, w2, 2)]
    halo_sends = [
        send(4, rows(r_in, 0, 16), rows(u, PAD + 528, 16), -1),
        send(5, rows(r_in, 496, 16), rows(u, PAD, 16), 1),
        send(6, rows(cr_in, 0, 8), rows(cr, PAD + 528, 8), -1),
        send(7, rows(cr_in, 504, 8), rows(cr, PAD + 8, 8), 1),
    ]
    help_r = [send(8, rows(r_in, 0, 16), rows(uh, PAD + 256, 16), -3),
              send(9, rows(r_in, 256, 256), rows(uh, PAD, 256), -2)]
    help_cr = [send(10, rows(cr_in, 0, 8), rows(crh, PAD + 256, 8), -3),
               send(11, rows(cr_in, 264, 248), rows(crh, PAD + 8, 248), -2)]
    front = [send(12, rows(cs_in, 240, 144), rows(cs, PAD, 144), 3),
             send(13, rows(cs_in, 384, 128), rows(cs, PAD + 144, 128), 3),
             send(14, rows(cs_in, 0, 32), rows(cs, PAD + 272, 32), 2)]
    back = send(15, rows(cs_in, 32, 240), rows(cs, PAD + 304, 240), 2)
    sends = mortar_sends + halo_sends + [help_r[0], help_cr[0], help_r[1], front[2], front[0], front[1], help_cr[1], back]

    nothing = jnp.zeros((PAD, W), F32)
    for ref, size in ((u, EXT), (v, EXT), (v2, EXT), (uh, HELP), (vh, HELP), (vh2, HELP)):
        ref[0:PAD] = nothing
        ref[PAD + size : PAD + size + PAD] = nothing
    for ref in (im, se, se2, imh, seh):
        ref[...] = jnp.zeros(ref.shape, F32)

    eye = jnp.where(lax.broadcasted_iota(jnp.int32, (128, 128), 0)
                    == lax.broadcasted_iota(jnp.int32, (128, 128), 1), 1.0, 0.0).astype(F32)

    def mortar(index, piece, size, base, m, w):
        _, n, _, line, place = piece
        low, span = window(piece, size)

        def lanes(ref):
            row = ref[line : line + 1, :]
            return (pltpu.roll(row, 128 - place, 1) if place else row)[:, :n]

        spot, weights = lanes(m) - base, lanes(w)
        spot = jnp.where(spot < 0, spot + NROWS, spot)
        spot = jnp.where(spot >= NROWS, spot - NROWS, spot)
        row = lax.broadcasted_iota(jnp.int32, (span, n), 0) + low
        pt = jnp.where(row == spot, weights, 0.0) + jnp.where(row == spot + 1, 1.0 - weights, 0.0)
        give[index][...] = pt
        take[index][...] = lax.dot_general(eye[:n, :n], pt, (((1,), (1,)), ((), ())), precision=HIGH,
                                           preferred_element_type=F32)

    own[0].wait()
    own[1].wait()
    for n, piece in enumerate(OWN):
        mortar(7 + n, piece, HELP, lax.rem(circ * ROWS + 1280, NROWS), m0, w0)
    pl.semaphore_wait(barrier, len(greeted))
    for copy in sends:
        copy.start()

    def spread(n):
        for offset in ((2, 0, 0, 0, 0), (10, 0, 0, 0, 0)):
            pl.semaphore_signal(token.at[n], inc=1, device_id=at(offset), device_id_type=MESH)

    spread(0)

    col = lax.broadcasted_iota(jnp.int32, (1, W), 1)
    not_first = col > 0
    not_last = col < W - 1

    def around(ref, start, n):
        mid = ref[pl.ds(start, n)]
        beside = (jnp.where(not_first, pltpu.roll(mid, 1, 1), 0.0)
                  + jnp.where(not_last, pltpu.roll(mid, W - 1, 1), 0.0))
        return mid, 0.25 * (ref[pl.ds(start - 1, n)] + ref[pl.ds(start + 1, n)] + beside)

    def project(src, dst, index, piece, size):
        low, span = window(piece, size)
        dst[pl.ds(PAD + piece[0], piece[1])] = jnp.dot(
            take[index][...], src[pl.ds(PAD + low, span)], precision=HIGH, preferred_element_type=F32)

    def give_back(src, coef, dst, index, piece, size):
        low, span = window(piece, size)
        mid, rest = around(src, PAD + piece[0], piece[1])
        response = coef[pl.ds(PAD + piece[0], piece[1])] * mid - rest
        dst[pl.ds(PAD + low, span)] += jnp.dot(
            give[index][...], response, precision=HIGH, preferred_element_type=F32)

    def rotor_part(src, coef, dst, first, end):
        for start in range(first, end, 128):
            n = min(128, end - start)
            mid, rest = around(src, PAD + start, n)
            dst[pl.ds(PAD + start, n)] += coef[pl.ds(PAD + start, n)] * mid - rest

    def add_products(parts, b_ref, p_ref, s_ref, first, end):
        for start in range(first, end, 16):
            at_rows = pl.ds(PAD + start, 16)
            b, p, s = b_ref[at_rows], p_ref[at_rows], s_ref[at_rows]
            for n, product in enumerate((b * p, b * s, p * p, p * s, s * s)):
                parts[n] = parts[n] + (product[:8] + product[8:])
        return parts

    pl.semaphore_wait(token.at[0], 2)
    spread(1)
    for copy in mortar_sends:
        copy.wait_recv()
    base = circ * ROWS - 16
    for n, piece in enumerate(FRONT + BACK):
        mortar(n, piece, EXT, base, *((m3, w3) if piece[2] == 3 else (m2, w2)))
    for copy in own[2:]:
        copy.wait()
    for copy in halo_sends:
        copy.wait_recv()
    for n, piece in enumerate(FRONT + BACK):
        project(u, v, n, piece, EXT)
    rotor_part(u, cr, im, 8, 536)

    pl.semaphore_wait(token.at[1], 2)
    for copy in help_r:
        copy.wait_recv()
    for n, piece in enumerate(OWN):
        project(uh, vh, 7 + n, piece, HELP)
    for n, piece in enumerate(OWN):
        give_back(vh, csh, imh, 7 + n, piece, HELP)

    for copy in help_cr:
        copy.wait_recv()
    rotor_part(uh, crh, imh, 8, 264)
    for n, piece in enumerate(OWN):
        project(imh, vh2, 7 + n, piece, HELP)
    rotor_part(imh, crh, seh, 16, 256)
    for n, piece in enumerate(OWN):
        give_back(vh2, csh, seh, 7 + n, piece, HELP)
    parts = add_products([jnp.zeros((8, W), F32)] * 5, uh, imh, seh, 16, 256)

    front[2].wait_recv()
    give_back(v, cs, im, 3, FRONT[3], EXT)
    front[0].wait_recv()
    give_back(v, cs, im, 0, FRONT[0], EXT)
    give_back(v, cs, im, 1, FRONT[1], EXT)
    front[1].wait_recv()
    give_back(v, cs, im, 2, FRONT[2], EXT)
    for n, piece in enumerate(FRONT):
        project(im, v2, n, piece, EXT)
    rotor_part(im, cr, se, 16, 16 + CUT)
    for n, piece in enumerate(FRONT):
        give_back(v2, cs, se, n, piece, EXT)
    parts = add_products(parts, u, im, se, 16, 16 + CUT)

    lane = lax.broadcasted_iota(jnp.int32, (1, 128), 1)
    total = jnp.zeros((1, 128), F32)
    for n, part in enumerate(parts):
        line = jnp.sum(part[:, :128] + part[:, 128:], axis=0, keepdims=True)
        total = jnp.where(lane == n, jnp.sum(line, axis=1, keepdims=True), total)

    def late():
        back.wait_recv()
        for n, piece in enumerate(BACK):
            give_back(v, cs, im, 4 + n, piece, EXT)
        for n, piece in list(enumerate(FRONT + BACK))[3:]:
            project(im, v2, n, piece, EXT)
        rotor_part(im, cr, se2, 16 + CUT, 528)
        for n, piece in list(enumerate(FRONT + BACK))[3:]:
            give_back(v2, cs, se2, n, piece, EXT)
        image_out[...] = im[PAD + 16 : PAD + 528]
        second_out[:CUT] = se[PAD + 16 : PAD + 16 + CUT]
        second_out[CUT:] = se2[PAD + 16 + CUT : PAD + 528]

    done = 0
    for stage, (partners, got) in enumerate(((X_PARTNERS, from_x), (Y_PARTNERS, from_y), (Z_PARTNERS, from_z))):
        mine[stage] = total
        copies = [
            pltpu.make_async_remote_copy(
                src_ref=mine.at[stage], dst_ref=got.at[pl.ds(n, 1)],
                send_sem=ar_send.at[done + n], recv_sem=ar_recv.at[done + n],
                device_id=at(offset), device_id_type=MESH)
            for n, offset in enumerate(partners)
        ]
        done += len(partners)
        for copy in copies:
            copy.start()
        if stage == 2:
            late()
        for copy in copies:
            copy.wait()
        total = total + jnp.sum(got[0 : len(partners)], axis=0, keepdims=True)

    def pick(n):
        return jnp.sum(jnp.where(lane == n, total, 0.0), axis=1, keepdims=True)

    cross_one, cross_two, gram_pp, gram_pq, gram_qq = [pick(n) for n in range(5)]
    determinant = gram_pp * gram_qq - gram_pq * gram_pq
    y1 = (gram_qq * cross_one - gram_pq * cross_two) / determinant
    y2 = (gram_pp * cross_two - gram_pq * cross_one) / determinant
    y1_out[...] = jnp.broadcast_to(y1, (1, W))
    y2_out[...] = jnp.broadcast_to(y2, (1, W))
    for copy in sends:
        copy.wait_send()


def local(right_side, coef_rotor, coef_stator, mortar_rows, mortar_weight):
    main = pltpu.VMEM((PAD + EXT + PAD, W), F32)
    helper = pltpu.VMEM((PAD + HELP + PAD, W), F32)
    hbm = pl.BlockSpec(memory_space=pltpu.HBM)
    vmem = pl.BlockSpec(memory_space=pltpu.VMEM)
    image, second, y1, y2 = pl.pallas_call(
        kernel,
        out_shape=(pltpu.VMEM((ROWS, W), F32), pltpu.VMEM((ROWS, W), F32), pltpu.VMEM((1, W), F32), pltpu.VMEM((1, W), F32)),
        in_specs=[hbm] * 5,
        out_specs=(vmem,) * 4,
        scratch_shapes=[main] * 8
        + [helper] * 7
        + [pltpu.VMEM((4, 128), jnp.int32)] * 3
        + [pltpu.VMEM((4, 128), F32)] * 3
        + [pltpu.VMEM((3, 1, 128), F32), pltpu.VMEM((8, 128), F32), pltpu.VMEM((8, 128), F32), pltpu.VMEM((16, 128), F32)]
        + [pltpu.SemaphoreType.DMA((n,)) for n in (5, N_SENDS, N_SENDS, 25, 25)]
        + [pltpu.SemaphoreType.REGULAR((2,))]
        + [pltpu.VMEM(s, F32) for s in SHAPES]
        + [pltpu.VMEM(s[::-1], F32) for s in SHAPES],
        compiler_params=pltpu.CompilerParams(collective_id=0, has_side_effects=True),
    )(right_side, coef_rotor, coef_stator, mortar_rows.reshape(4, 128), mortar_weight.reshape(4, 128))
    return y1 * right_side + y2 * image, right_side - y1 * image - y2 * second


def solution(mesh):
    finer = Mesh(mesh.devices.reshape(SIZES), AXES)
    circ, radax = AXES[:2], AXES[2:]
    whole = P(circ, radax)
    return jax.shard_map(local, mesh=finer, in_specs=(whole, whole, whole, P(circ), P(circ)),
                         out_specs=(whole, whole), check_vma=False)
```

time: 61.2 us -> 52.3 us (0.85); the launches traced: 60.9 us -> 51.3 us
  Pallas kernels: 57.2 us -> 49.5 us
  other arithmetic: 2.29 us -> 1.14 us
  local copies, waits for them, and re-layouts: 0.72 us -> 0.01 us
    pallas_call x1, Pallas kernels: 57.2 us -> 49.5 us  [local(): pl.pallas_call(kernel, out_shape=(pltpu.VMEM((ROWS, W), F32), pltpu.VMEM(...]
    sub x1, other arithmetic: 2.29 us -> 1.14 us  [local(): return (y1 * right_side + y2 * image, right_side - y1 * image - y2 * second)]
    slice x1 -> x0, local copies, waits for them, and re-layouts: 0.72 us -> none  [local(): y1, y2 = (y[0:1], y[8:9])]
where the time goes in v2:
time: 52.3 us; the launch traced here: 51.3 us
  Pallas kernels  49.5 us (95%)
  other arithmetic  1.14 us (2%)
  between operations  0.65 us (1%)
    pallas_call x1, Pallas kernels, local(): pl.pallas_call(kernel, out_shape=(pltpu.VMEM((ROWS, W), F32), pltpu.VMEM(...  49.5 us
    sub x1, other arithmetic, local(): return (y1 * right_side + y2 * image, right_side - y1 * image - y2 * second)  1.14 us

profile of v2, /device:TPU:1, one launch (start us, length us, event | category | flops | bytes accessed | tf_op | source)
XLA Modules:
  0.0 51.3 jit_solution(3358587498288050476)
XLA Ops:
  0.6 0.0 copy-start
  0.6 49.5 %shard_map.68 = (f32[512,256]{1,0:T(8,128)S(1)}, f32[512,256]{1,0:T(8,128)S(1)}, f32[1,256]{1,0:T(1,128)S(1)}, f32[1,256]{1,0:T(1,128)S(1)}) custom-call(f32[512,256]{1,0:T(8,128)} %r_in.1, f32[512,256]{1,0:T(8,128)} %cr_in.1, f32[512,256]{1,0:T(8,128)} %cs_in.1, s32[4,128]{1,0:T(4,128)} %bitcast.6, f32[4,128]{1,0:T(4,128)} %bitcast.7), custom_call_target="tpu_custom_call" | custom-call | tf_op jit(solution)/shard_map/pallas_call | solution.py:276
  50.1 0.0 copy-done
  50.2 1.1 %multiply_subtract_fusion = (f32[512,256]{1,0:T(8,128)}, f32[512,256]{1,0:T(8,128)}) fusion(f32[512,256]{1,0:T(8,128)S(1)} %get-tuple-element.9, f32[512,256]{1,0:T(8,128)S(1)} %copy-done, f32[512,256]{1,0:T(8,128)S(1)} %get-tuple-element.8, f32[256]{0:T(256)S(1)} %bitcast.5, f32[256]{0:T(256)S(1)} %bitcast.4), kind=kLoop, calls=%fused_computation | loop fusion | flops 917504 | bytes 2623488 | tf_op jit(solution)/shard_map/sub | solution.py:292
Async XLA Ops:
  0.6 49.5 %copy-start = (f32[512,256]{1,0:T(8,128)S(1)}, f32[512,256]{1,0:T(8,128)}, u32[]{:S(2)}) copy-start(f32[512,256]{1,0:T(8,128)} %r_in.1) | copy-start | bytes 1572868

commit v3 on v2

--- a/solution.py
+++ b/solution.py
@@ -14,20 +14,23 @@
 NROWS = CIRC * ROWS
 PAD = 8
 EXT = 544
-CUT = 272
-HELP = 272
+CUT = 296
+HELP = 248
+RELAY = 64
 MESH = pl.DeviceIdType.MESH
 HIGH = lax.Precision.HIGHEST
 F32 = jnp.float32
 
-FRONT = [(0, 16, 3, 1, 112), (16, 128, 3, 2, 0), (144, 128, 3, 3, 0), (272, 32, 2, 0, 0)]
-BACK = [(304, 96, 2, 0, 32), (400, 128, 2, 1, 0), (528, 16, 2, 2, 0)]
-OWN = [(0, 128, 0, 0, 0), (128, 128, 0, 1, 0), (256, 16, 0, 2, 0)]
+FRONT = [(0, 16, 3, 1, 112), (16, 128, 3, 2, 0), (144, 16, 3, 3, 0), (160, 112, 3, 3, 16), (272, 56, 2, 0, 0)]
+BACK = [(328, 72, 2, 0, 56), (400, 128, 2, 1, 0), (528, 16, 2, 2, 0)]
+OWN = [(0, 104, 0, 0, 24), (104, 128, 0, 1, 0), (232, 16, 0, 2, 0)]
 X_PARTNERS = [(0, a, 0, b, k) for a in range(2) for b in range(2) for k in range(2) if a + b + k]
 Y_PARTNERS = [(0, 0, d, 0, 0) for d in range(1, 8)]
 Z_PARTNERS = [(d, 0, 0, 0, 0) for d in range(1, 12)]
 NEAR = [(d, a, 0, 0, 0) for d in (1, 2, 10, 11) for a in range(2)]
-N_SENDS = 16
+N_SENDS = 18
+FIRST_BACK = len(FRONT)
+FIRST_OWN = len(FRONT + BACK)
 
 
 def window(piece, size):
@@ -40,7 +43,7 @@
 
 def kernel(r_in, cr_in, cs_in, m_in, w_in, image_out, second_out, y1_out, y2_out,
            u, cr, cs, v, v2, im, se, se2, uh, crh, csh, vh, vh2, imh, seh,
-           m3, m2, m0, w3, w2, w0, mine, from_x, from_y, from_z,
+           relay, m3, m2, m0, w3, w2, w0, mine, from_x, from_y, from_z,
            local_sem, send_sem, recv_sem, ar_send, ar_recv, token, *matrices):
     me = [lax.axis_index(a) for a in AXES]
     circ = me[0] * 2 + me[1]
@@ -63,7 +66,7 @@
         pltpu.make_async_copy(w_in, w0, local_sem.at[1]),
         pltpu.make_async_copy(r_in, u.at[pl.ds(PAD + 16, ROWS)], local_sem.at[2]),
         pltpu.make_async_copy(cr_in, cr.at[pl.ds(PAD + 16, ROWS)], local_sem.at[3]),
-        pltpu.make_async_copy(cs_in.at[pl.ds(0, HELP)], csh.at[pl.ds(PAD, HELP)], local_sem.at[4]),
+        pltpu.make_async_copy(cs_in.at[pl.ds(24, HELP)], csh.at[pl.ds(PAD, HELP)], local_sem.at[4]),
     ]
     for copy in own:
         copy.start()
@@ -83,56 +86,59 @@
         send(6, rows(cr_in, 0, 8), rows(cr, PAD + 528, 8), -1),
         send(7, rows(cr_in, 504, 8), rows(cr, PAD + 8, 8), 1),
     ]
-    help_r = [send(8, rows(r_in, 0, 16), rows(uh, PAD + 256, 16), -3),
-              send(9, rows(r_in, 256, 256), rows(uh, PAD, 256), -2)]
-    help_cr = [send(10, rows(cr_in, 0, 8), rows(crh, PAD + 256, 8), -3),
-               send(11, rows(cr_in, 264, 248), rows(crh, PAD + 8, 248), -2)]
-    front = [send(12, rows(cs_in, 240, 144), rows(cs, PAD, 144), 3),
+    help_r = [send(8, rows(r_in, 0, 16), rows(uh, PAD + 232, 16), -3),
+              send(9, rows(r_in, 280, 232), rows(uh, PAD, 232), -2)]
+    help_cr = [send(10, rows(cr_in, 0, 8), rows(crh, PAD + 232, 8), -3),
+               send(11, rows(cr_in, 288, 224), rows(crh, PAD + 8, 224), -2)]
+    early = [send(12, rows(cs_in, 0, 56), rows(cs, PAD + 272, 56), 2),
              send(13, rows(cs_in, 384, 128), rows(cs, PAD + 144, 128), 3),
-             send(14, rows(cs_in, 0, 32), rows(cs, PAD + 272, 32), 2)]
-    back = send(15, rows(cs_in, 32, 240), rows(cs, PAD + 304, 240), 2)
-    sends = mortar_sends + halo_sends + [help_r[0], help_cr[0], help_r[1], front[2], front[0], front[1], help_cr[1], back]
-
+             send(14, rows(cs_in, 240 + RELAY, 144 - RELAY), rows(cs, PAD + RELAY, 144 - RELAY), 3)]
+    straight = send(15, rows(cs_in, 240, RELAY), rows(cs, PAD, RELAY), 3)
+    aside = send(16, rows(cs_in, 240, RELAY), relay, -1)
+    onward = pltpu.make_async_remote_copy(
+        src_ref=relay, dst_ref=rows(cs, PAD, RELAY), send_sem=send_sem.at[16], recv_sem=recv_sem.at[15],
+        device_id=along(4), device_id_type=MESH)
+    back = send(17, rows(cs_in, 56, 216), rows(cs, PAD + 328, 216), 2)
+    odd = me[1] == 1
+    sends = mortar_sends + halo_sends + [help_r[0], help_cr[0], help_r[1]] + early + [help_cr[1]]
+
+    def mortar(index, piece, size, base, m, w):
+        _, n, _, line, place = piece
+        low, span = window(piece, size)
+
+        def lanes(ref):
+            row = ref[line : line + 1, :]
+            return (pltpu.roll(row, 128 - place, 1) if place else row)[:, :n]
+
+        spot, weights = lanes(m) - base, lanes(w)
+        spot = jnp.where(spot < 0, spot + NROWS, spot)
+        spot = jnp.where(spot >= NROWS, spot - NROWS, spot)
+        row = lax.broadcasted_iota(jnp.int32, (span, n), 0) + low
+        pt = jnp.where(row == spot, weights, 0.0) + jnp.where(row == spot + 1, 1.0 - weights, 0.0)
+        give[index][...] = pt
+        take[index][...] = jnp.transpose(pt)
+
+    pl.semaphore_wait(barrier, len(greeted))
+    pl.when(odd)(aside.start)
+    for copy in sends:
+        copy.start()
+    pl.when(jnp.logical_not(odd))(straight.start)
+
+    def spread(n):
+        for offset in ((2, 0, 0, 0, 0), (10, 0, 0, 0, 0)):
+            pl.semaphore_signal(token.at[n], inc=1, device_id=at(offset), device_id_type=MESH)
+
+    spread(0)
     nothing = jnp.zeros((PAD, W), F32)
     for ref, size in ((u, EXT), (v, EXT), (v2, EXT), (uh, HELP), (vh, HELP), (vh2, HELP)):
         ref[0:PAD] = nothing
         ref[PAD + size : PAD + size + PAD] = nothing
     for ref in (im, se, se2, imh, seh):
         ref[...] = jnp.zeros(ref.shape, F32)
-
-    eye = jnp.where(lax.broadcasted_iota(jnp.int32, (128, 128), 0)
-                    == lax.broadcasted_iota(jnp.int32, (128, 128), 1), 1.0, 0.0).astype(F32)
-
-    def mortar(index, piece, size, base, m, w):
-        _, n, _, line, place = piece
-        low, span = window(piece, size)
-
-        def lanes(ref):
-            row = ref[line : line + 1, :]
-            return (pltpu.roll(row, 128 - place, 1) if place else row)[:, :n]
-
-        spot, weights = lanes(m) - base, lanes(w)
-        spot = jnp.where(spot < 0, spot + NROWS, spot)
-        spot = jnp.where(spot >= NROWS, spot - NROWS, spot)
-        row = lax.broadcasted_iota(jnp.int32, (span, n), 0) + low
-        pt = jnp.where(row == spot, weights, 0.0) + jnp.where(row == spot + 1, 1.0 - weights, 0.0)
-        give[index][...] = pt
-        take[index][...] = lax.dot_general(eye[:n, :n], pt, (((1,), (1,)), ((), ())), precision=HIGH,
-                                           preferred_element_type=F32)
-
     own[0].wait()
     own[1].wait()
     for n, piece in enumerate(OWN):
-        mortar(7 + n, piece, HELP, lax.rem(circ * ROWS + 1280, NROWS), m0, w0)
-    pl.semaphore_wait(barrier, len(greeted))
-    for copy in sends:
-        copy.start()
-
-    def spread(n):
-        for offset in ((2, 0, 0, 0, 0), (10, 0, 0, 0, 0)):
-            pl.semaphore_signal(token.at[n], inc=1, device_id=at(offset), device_id_type=MESH)
-
-    spread(0)
+        mortar(FIRST_OWN + n, piece, HELP, lax.rem(circ * ROWS + 1304, NROWS), m0, w0)
 
     col = lax.broadcasted_iota(jnp.int32, (1, W), 1)
     not_first = col > 0
@@ -163,11 +169,11 @@
             dst[pl.ds(PAD + start, n)] += coef[pl.ds(PAD + start, n)] * mid - rest
 
     def add_products(parts, b_ref, p_ref, s_ref, first, end):
-        for start in range(first, end, 16):
-            at_rows = pl.ds(PAD + start, 16)
+        for start in range(first, end, 8):
+            at_rows = pl.ds(PAD + start, 8)
             b, p, s = b_ref[at_rows], p_ref[at_rows], s_ref[at_rows]
             for n, product in enumerate((b * p, b * s, p * p, p * s, s * s)):
-                parts[n] = parts[n] + (product[:8] + product[8:])
+                parts[n] = parts[n] + product
         return parts
 
     pl.semaphore_wait(token.at[0], 2)
@@ -175,47 +181,78 @@
     for copy in mortar_sends:
         copy.wait_recv()
     base = circ * ROWS - 16
-    for n, piece in enumerate(FRONT + BACK):
+
+    def prepare(n):
+        piece = (FRONT + BACK)[n]
         mortar(n, piece, EXT, base, *((m3, w3) if piece[2] == 3 else (m2, w2)))
+
+    for n in range(FIRST_BACK + 1):
+        prepare(n)
     for copy in own[2:]:
         copy.wait()
     for copy in halo_sends:
         copy.wait_recv()
-    for n, piece in enumerate(FRONT + BACK):
-        project(u, v, n, piece, EXT)
-    rotor_part(u, cr, im, 8, 536)
-
+    for n in range(FIRST_BACK + 1):
+        project(u, v, n, (FRONT + BACK)[n], EXT)
+    rotor_part(u, cr, im, 8, 328)
+
+    @pl.when(jnp.logical_not(odd))
+    def _():
+        aside.wait_recv()
+        onward.start()
+
+    back.start()
     pl.semaphore_wait(token.at[1], 2)
     for copy in help_r:
         copy.wait_recv()
     for n, piece in enumerate(OWN):
-        project(uh, vh, 7 + n, piece, HELP)
-    for n, piece in enumerate(OWN):
-        give_back(vh, csh, imh, 7 + n, piece, HELP)
-
+        project(uh, vh, FIRST_OWN + n, piece, HELP)
+    for n, piece in enumerate(OWN):
+        give_back(vh, csh, imh, FIRST_OWN + n, piece, HELP)
+
+    def first(n):
+        give_back(v, cs, im, n, FRONT[n], EXT)
+
+    def look(n):
+        project(im, v2, n, FRONT[n], EXT)
+
+    def then(n):
+        give_back(v2, cs, se, n, FRONT[n], EXT)
+
+    early[0].wait_recv()
+    first(4)
+    early[1].wait_recv()
+    first(2)
+    first(3)
+    look(4)
+    look(3)
+    look(2)
+    rotor_part(im, cr, se, 168, 16 + CUT)
+    then(4)
+    then(3)
+    parts = add_products([jnp.zeros((8, W), F32)] * 5, u, im, se, 168, 16 + CUT)
     for copy in help_cr:
         copy.wait_recv()
-    rotor_part(uh, crh, imh, 8, 264)
-    for n, piece in enumerate(OWN):
-        project(imh, vh2, 7 + n, piece, HELP)
-    rotor_part(imh, crh, seh, 16, 256)
-    for n, piece in enumerate(OWN):
-        give_back(vh2, csh, seh, 7 + n, piece, HELP)
-    parts = add_products([jnp.zeros((8, W), F32)] * 5, uh, imh, seh, 16, 256)
-
-    front[2].wait_recv()
-    give_back(v, cs, im, 3, FRONT[3], EXT)
-    front[0].wait_recv()
-    give_back(v, cs, im, 0, FRONT[0], EXT)
-    give_back(v, cs, im, 1, FRONT[1], EXT)
-    front[1].wait_recv()
-    give_back(v, cs, im, 2, FRONT[2], EXT)
-    for n, piece in enumerate(FRONT):
-        project(im, v2, n, piece, EXT)
-    rotor_part(im, cr, se, 16, 16 + CUT)
-    for n, piece in enumerate(FRONT):
-        give_back(v2, cs, se, n, piece, EXT)
-    parts = add_products(parts, u, im, se, 16, 16 + CUT)
+    rotor_part(uh, crh, imh, 8, 240)
+    for n, piece in enumerate(OWN):
+        project(imh, vh2, FIRST_OWN + n, piece, HELP)
+    rotor_part(imh, crh, seh, 16, 232)
+    for n, piece in enumerate(OWN):
+        give_back(vh2, csh, seh, FIRST_OWN + n, piece, HELP)
+    parts = add_products(parts, uh, imh, seh, 16, 232)
+
+    early[2].wait_recv()
+    straight.wait_recv()
+    first(1)
+    first(0)
+    look(0)
+    look(1)
+    look(2)
+    rotor_part(im, cr, se, 16, 168)
+    then(0)
+    then(1)
+    then(2)
+    parts = add_products(parts, u, im, se, 16, 168)
 
     lane = lax.broadcasted_iota(jnp.int32, (1, 128), 1)
     total = jnp.zeros((1, 128), F32)
@@ -224,13 +261,17 @@
         total = jnp.where(lane == n, jnp.sum(line, axis=1, keepdims=True), total)
 
     def late():
+        for n in (FIRST_BACK + 1, FIRST_BACK + 2):
+            prepare(n)
+            project(u, v, n, (FRONT + BACK)[n], EXT)
+        rotor_part(u, cr, im, 328, 536)
         back.wait_recv()
         for n, piece in enumerate(BACK):
-            give_back(v, cs, im, 4 + n, piece, EXT)
-        for n, piece in list(enumerate(FRONT + BACK))[3:]:
+            give_back(v, cs, im, FIRST_BACK + n, piece, EXT)
+        for n, piece in list(enumerate(FRONT + BACK))[FIRST_BACK - 1 :]:
             project(im, v2, n, piece, EXT)
         rotor_part(im, cr, se2, 16 + CUT, 528)
-        for n, piece in list(enumerate(FRONT + BACK))[3:]:
+        for n, piece in list(enumerate(FRONT + BACK))[FIRST_BACK - 1 :]:
             give_back(v2, cs, se2, n, piece, EXT)
         image_out[...] = im[PAD + 16 : PAD + 528]
         second_out[:CUT] = se[PAD + 16 : PAD + 16 + CUT]
@@ -266,6 +307,13 @@
     y2_out[...] = jnp.broadcast_to(y2, (1, W))
     for copy in sends:
         copy.wait_send()
+    back.wait_send()
+    pl.when(odd)(aside.wait_send)
+
+    @pl.when(jnp.logical_not(odd))
+    def _():
+        straight.wait_send()
+        onward.wait_send()
 
 
 def local(right_side, coef_rotor, coef_stator, mortar_rows, mortar_weight):
@@ -280,6 +328,7 @@
         out_specs=(vmem,) * 4,
         scratch_shapes=[main] * 8
         + [helper] * 7
+        + [pltpu.VMEM((RELAY, W), F32)]
         + [pltpu.VMEM((4, 128), jnp.int32)] * 3
         + [pltpu.VMEM((4, 128), F32)] * 3
         + [pltpu.VMEM((3, 1, 128), F32), pltpu.VMEM((8, 128), F32), pltpu.VMEM((8, 128), F32), pltpu.VMEM((16, 128), F32)]

time: 52.3 us -> 50.2 us (0.960)
  Pallas kernels: 49.5 us -> 47.5 us
    pallas_call x1, Pallas kernels: 49.5 us -> 47.5 us  [local(): pl.pallas_call(kernel, out_shape=(pltpu.VMEM((ROWS, W), F32), pltpu.VMEM(...]
where the time goes in v3:
time: 50.2 us; the launch traced here: 49.3 us
  Pallas kernels  47.5 us (95%)
  other arithmetic  1.14 us (2%)
  between operations  0.65 us (1%)
    pallas_call x1, Pallas kernels, local(): pl.pallas_call(kernel, out_shape=(pltpu.VMEM((ROWS, W), F32), pltpu.VMEM(...  47.5 us
    sub x1, other arithmetic, local(): return (y1 * right_side + y2 * image, right_side - y1 * image - y2 * second)  1.14 us

profile of v3, /device:TPU:1, one launch (start us, length us, event | category | flops | bytes accessed | tf_op | source)
XLA Modules:
  0.0 49.3 jit_solution(16248707279556981689)
XLA Ops:
  0.6 0.0 copy-start
  0.6 47.5 %shard_map.68 = (f32[512,256]{1,0:T(8,128)S(1)}, f32[512,256]{1,0:T(8,128)S(1)}, f32[1,256]{1,0:T(1,128)S(1)}, f32[1,256]{1,0:T(1,128)S(1)}) custom-call(f32[512,256]{1,0:T(8,128)} %r_in.1, f32[512,256]{1,0:T(8,128)} %cr_in.1, f32[512,256]{1,0:T(8,128)} %cs_in.1, s32[4,128]{1,0:T(4,128)} %bitcast.6, f32[4,128]{1,0:T(4,128)} %bitcast.7), custom_call_target="tpu_custom_call" | custom-call | tf_op jit(solution)/shard_map/pallas_call | solution.py:324
  48.2 0.0 copy-done
  48.2 1.1 %multiply_subtract_fusion = (f32[512,256]{1,0:T(8,128)}, f32[512,256]{1,0:T(8,128)}) fusion(f32[512,256]{1,0:T(8,128)S(1)} %get-tuple-element.9, f32[512,256]{1,0:T(8,128)S(1)} %copy-done, f32[512,256]{1,0:T(8,128)S(1)} %get-tuple-element.8, f32[256]{0:T(256)S(1)} %bitcast.5, f32[256]{0:T(256)S(1)} %bitcast.4), kind=kLoop, calls=%fused_computation | loop fusion | flops 917504 | bytes 2623488 | tf_op jit(solution)/shard_map/sub | solution.py:341
Async XLA Ops:
  0.6 47.6 %copy-start = (f32[512,256]{1,0:T(8,128)S(1)}, f32[512,256]{1,0:T(8,128)}, u32[]{:S(2)}) copy-start(f32[512,256]{1,0:T(8,128)} %r_in.1) | copy-start | bytes 1572868
